TPU v7x, 32 devices: a whole 2x2x4 slice. The times are simulated.
32 devices in a mesh: sub: 8 (over z, x), crs: 4 (over y, core).
Axes of the slice: x: 2, y: 2, z: 4, core: 2. Of those that a mesh axis runs over, the one named last changes fastest.
Arguments:
- schur_block: float32 [64, 1536, 1536], P('sub', 'crs'), as said below
- rigid_modes: float32 [64, 6, 1536], P('sub'), may hold values from -0.4375 to 0.4375
- coarse_inverse: float32 [384, 384], P('crs'), as said below
- dual_rhs: float32 [32, 64, 1536], P('crs', 'sub'), may hold values from -6 to 6
- stiff_diag: float32 [64, 1536], P('sub'), may hold values from 0.25 to 2.5
- face_length: int32 [64, 6], P('sub'), may hold values from 0 to 256, as said below
Outputs:
- multipliers: float32 [32, 64, 1536], P('crs', 'sub')
- projected: float32 [32, 64, 1536], P('crs', 'sub')
Inputs may be any that keep to these rules, and one draw needn't show every extreme that they name: Equal on the two sides of a face: face_length[s, c] = face_length[partner(s, c), c]; 0 where partner(s, c) does not exist; at least 64 where it exists. Each schur_block[s] is symmetric positive definite. coarse_inverse is symmetric.
All inputs are finite; a program needn't handle non-finite values.
Results may differ from a plain program's by a relative error of at most 0.0003.
Values sent between devices are 32-bit elements; how exact they have to be, the bound alone decides.
A program may use at most 64 MiB of HBM per device.

v0:
```python
import functools

import jax
import jax.numpy as jnp
import numpy as np
from jax import lax
from jax.experimental import pallas as pl
from jax.experimental.pallas import tpu as pltpu
from jax.sharding import PartitionSpec as P

ITERS = 2
SY = 2
SZ = 4
SUBS = 8

PRECISE = lax.Precision.HIGHEST
SPLIT = lax.Precision.HIGH


def local_lookup():
    indices = np.arange(SUBS)
    coords = [indices // SZ, indices % SZ]
    extent = [SY, SZ]
    stride = [SZ, 1]
    lookup = np.zeros((4, SUBS), np.int32)
    for colour in range(4):
        axis_pick = colour // 2
        anchor = coords[axis_pick]
        offset = np.where(anchor % 2 == colour % 2, 1, -1)
        target = anchor + offset
        inside = (target >= 0) & (target < extent[axis_pick])
        lookup[colour] = np.where(inside, indices + offset * stride[axis_pick], indices)
    return lookup


def by_collectives(schur_block, rigid_modes, coarse_inverse, dual_rhs, stiff_diag, face_length):
    loads, subs, interface = dual_rhs.shape
    slot = interface // 6
    modes = rigid_modes.shape[1]
    own = subs * modes
    nsub = lax.axis_size("sub")
    sub_index = lax.axis_index("sub")
    even = sub_index % 2 == 0
    lookup = local_lookup()
    positions = jnp.arange(interface) % slot
    usable = (jnp.repeat(face_length, slot, axis=1) > positions[None, :]).astype(jnp.float32)
    up = [(i, i + 1) for i in range(nsub - 1)]
    down = [(i + 1, i) for i in range(nsub - 1)]

    def partner(vector):
        first = vector[..., :slot]
        second = vector[..., slot : 2 * slot]
        from_left = lax.ppermute(jnp.where(even, first, second), "sub", up)
        from_right = lax.ppermute(jnp.where(even, second, first), "sub", down)
        pieces = [jnp.where(even, from_right, from_left), jnp.where(even, from_left, from_right)]
        for colour in range(2, 6):
            window = vector[..., colour * slot : (colour + 1) * slot]
            pieces.append(
                jnp.concatenate([window[..., t : t + 1, :] for t in lookup[colour - 2]], axis=-2)
            )
        return jnp.concatenate(pieces, axis=-1)

    modes_first = jnp.swapaxes(rigid_modes, 0, 1)
    together = jnp.concatenate([dual_rhs, modes_first, stiff_diag[None]], axis=0)
    across = partner(together)
    residual = usable * (dual_rhs - across[:loads])
    modes_across = across[loads : loads + modes]
    precond = usable * (stiff_diag + across[-1])

    inverse = lax.all_gather(coarse_inverse, "crs", axis=0, tiled=True)

    def by_slot(array):
        return array.reshape(array.shape[:-1] + (6, slot))

    basis = by_slot(usable * jnp.concatenate([modes_first, -modes_across], axis=0))

    weighted = by_slot(modes_first * precond)
    blocks = jnp.einsum("msck,nsck->scmn", weighted, basis, precision=PRECISE)
    total_subs = nsub * subs
    here = sub_index * subs + jnp.arange(subs)
    left = here - subs
    right = here + subs
    targets = [jnp.where(even, right, left), jnp.where(even, left, right)]
    for colour in range(2, 6):
        targets.append(sub_index * subs + jnp.asarray(lookup[colour - 2]))
    targets = jnp.stack(targets, axis=1)
    hot_across = (targets[:, :, None] == jnp.arange(total_subs)).astype(jnp.float32)
    hot_here = (here[:, None] == jnp.arange(total_subs)).astype(jnp.float32)
    dense = jnp.einsum("smn,st->smtn", blocks[..., :modes].sum(axis=1), hot_here, precision=PRECISE)
    dense = dense + jnp.einsum("scmn,sct->smtn", blocks[..., modes:], hot_across, precision=PRECISE)
    dense = dense.reshape(own, total_subs * modes)
    middle = lax.all_gather(dense, "sub", axis=0, tiled=True)

    def coarse(vector):
        return jnp.einsum("lsi,msi->lsm", vector, modes_first, precision=PRECISE).reshape(loads, own)

    def dots(a, b):
        return jnp.sum(a * b, axis=(1, 2))[:, None]

    def shared(parts):
        gathered = lax.all_gather(jnp.concatenate(parts, axis=1), "sub", axis=0)
        count = own * (sum(part.shape[1] == own for part in parts))
        outs = []
        for at in range(0, count, own):
            outs.append(jnp.swapaxes(gathered[:, :, at : at + own], 0, 1).reshape(loads, nsub * own))
        sums = jnp.sum(gathered[:, :, count:], axis=0)
        return outs, [sums[:, j : j + 1] for j in range(sums.shape[1])]

    def solve(values):
        return jnp.einsum("lb,ab->la", values, inverse, precision=PRECISE)

    def lifted(values):
        grid = values.reshape(loads, nsub, subs, modes)
        padded = jnp.pad(grid, ((0, 0), (1, 1), (0, 0), (0, 0)))
        near = lax.dynamic_slice_in_dim(padded, sub_index, 3, axis=1)
        before, mine, after = near[:, 0], near[:, 1], near[:, 2]
        pieces = [jnp.where(even, after, before), jnp.where(even, before, after)]
        for colour in range(2, 6):
            pieces.append(jnp.stack([mine[:, t] for t in lookup[colour - 2]], axis=1))
        other = jnp.stack(pieces, axis=2)
        mine = jnp.broadcast_to(mine[:, :, None], other.shape)
        factors = jnp.concatenate([mine, other], axis=-1)
        out = jnp.einsum("lscm,msck->lsck", factors, basis, precision=PRECISE)
        return out.reshape(loads, subs, interface)

    def direction(residual, c_res, c_scaled, power):
        y = solve(c_res)
        my = jnp.einsum("lb,ab->la", y, middle, precision=PRECISE)
        energy = 0.5 * power - 2.0 * jnp.sum(y * c_scaled, axis=1, keepdims=True)
        energy = energy + jnp.sum(y * my, axis=1, keepdims=True)
        t = solve(c_scaled - my)
        return precond * (residual - lifted(y)) - lifted(t), energy

    scaled = precond * residual
    (c_res, c_scaled), (power,) = shared([coarse(residual), coarse(scaled), dots(residual, scaled)])
    search, energy = direction(residual, c_res, c_scaled, power)
    multipliers = None
    for iteration in range(ITERS):
        by_rows = jnp.einsum(
            "sij,lsj->lsi",
            schur_block,
            lax.all_gather(search, "crs", axis=0, tiled=True),
            precision=SPLIT,
        )
        product = lax.all_to_all(by_rows, "crs", split_axis=0, concat_axis=2, tiled=True)
        image = usable * (product - partner(product))
        last = iteration + 1 == ITERS
        curve = dots(search, product)
        if last:
            (c_image,), (curve,) = shared([coarse(image), curve])
        else:
            scaled_image = precond * image
            parts = [
                coarse(image),
                coarse(scaled_image),
                curve,
                dots(residual, scaled_image),
                dots(image, scaled_image),
            ]
            (c_image, c_scaled_image), (curve, cross, square) = shared(parts)
        step = energy / curve
        moved = step[:, :, None] * search
        multipliers = moved if multipliers is None else multipliers + moved
        residual = residual - step[:, :, None] * image
        c_res = c_res - step * c_image
        if last:
            projected = residual - lifted(solve(c_res))
        else:
            c_scaled = c_scaled - step * c_scaled_image
            power = power - 2.0 * step * cross + step * step * square
            fresh, energy_new = direction(residual, c_res, c_scaled, power)
            search = fresh + (energy_new / energy)[:, :, None] * search
            energy = energy_new
    return (multipliers, projected)


MESH = pl.DeviceIdType.MESH


def across_rows(a, b, precision=None):
    return lax.dot_general(
        a, b, (((1,), (1,)), ((), ())), precision=precision, preferred_element_type=jnp.float32
    )


def halves(x):
    high = x.astype(jnp.bfloat16)
    return high, (x - high.astype(jnp.float32)).astype(jnp.bfloat16)


def operate_kernel(
    nsub,
    lookup,
    schur,
    search,
    usable,
    image,
    curve,
    hold,
    gath,
    res,
    product,
    across,
    load_sem,
    gsend,
    grecv,
    asend,
    arecv,
    osem,
    fsend,
    frecv,
):
    subs, loads, interface = search.shape
    rows = hold.shape[1]
    slot = interface // 6
    me = lax.axis_index("sub")
    q = lax.axis_index("crs")
    core = q % 2
    twin = q + 1 - 2 * core
    far = (q + 2) % 4
    diagonal = (twin + 2) % 4
    odd = me % 2
    first = me + 1 - 2 * odd
    second = me - 1 + 2 * odd
    has_second = jnp.logical_and(second >= 0, second < nsub)

    def load(s):
        return pltpu.make_async_copy(schur.at[s], hold.at[s], load_sem.at[s])

    def start_load(s, carry):
        load(s).start()
        return carry

    lax.fori_loop(0, subs, start_load, 0)
    barrier = pltpu.get_barrier_semaphore()
    for peer in (twin, far, diagonal):
        pl.semaphore_signal(barrier, inc=1, device_id=(me, peer), device_id_type=MESH)
    pl.semaphore_signal(barrier, inc=1, device_id=(first, q), device_id_type=MESH)

    @pl.when(has_second)
    def _():
        pl.semaphore_signal(barrier, inc=1, device_id=(second, q), device_id_type=MESH)

    pl.semaphore_wait(barrier, jnp.where(has_second, 5, 4))

    def remote(src, dst, send, recv, target):
        return pltpu.make_async_remote_copy(
            src_ref=src,
            dst_ref=dst,
            send_sem=send,
            recv_sem=recv,
            device_id=target,
            device_id_type=MESH,
        )

    def to_twin(s, block):
        return remote(search.at[s], gath.at[s, block], gsend.at[0, s], grecv.at[0, s], (me, twin))

    def to_far(s, block):
        return remote(search.at[s], gath.at[s, block], gsend.at[1, s], grecv.at[1, s], (me, far))

    def relay(s, source, block):
        return remote(
            gath.at[s, source], gath.at[s, block], gsend.at[2, s], grecv.at[2, s], (me, twin)
        )

    def spread(s, carry):
        to_far(s, q).start()
        to_twin(s, q).start()
        return carry

    lax.fori_loop(0, subs, spread, 0)
    gath[:, q] = search[...]

    def forward(s):
        to_far(s, far).wait_recv()
        relay(s, far, far).start()

    peers = (twin, far, diagonal)
    own_columns = pl.ds(pl.multiple_of(q * rows, 128), rows)

    def give(s, j):
        return remote(
            res.at[s, peers[j]],
            product.at[s, :, own_columns],
            asend.at[j, s],
            arecv.at[j, s],
            (me, peers[j]),
        )

    def taken(s, j):
        columns = pl.ds(pl.multiple_of(peers[j] * rows, 128), rows)
        return remote(
            res.at[s, peers[j]],
            product.at[s, :, columns],
            asend.at[j, s],
            arecv.at[j, s],
            (me, peers[j]),
        )

    def keep(s):
        return pltpu.make_async_copy(res.at[s, q], product.at[s, :, own_columns], osem.at[s])

    forward(0)

    def multiply(s, carry):
        @pl.when(s + 1 < subs)
        def _():
            forward(s + 1)

        load(s).wait()
        w_high, w_low = halves(hold[s])
        to_twin(s, twin).wait_recv()
        relay(s, far, diagonal).wait_recv()
        x_high, x_low = halves(gath[s].reshape(4 * loads, interface))
        both = across_rows(jnp.concatenate([x_high, x_low], axis=0), w_high)
        out = both[: 4 * loads] + both[4 * loads :] + across_rows(x_high, w_low)
        res[s] = out.reshape(4, loads, rows)
        for j in range(3):
            give(s, j).start()
        keep(s).start()
        return carry

    lax.fori_loop(0, subs, multiply, 0)

    def finish(s, carry):
        keep(s).wait()
        for j in range(3):
            taken(s, j).wait_recv()
        return carry

    lax.fori_loop(0, subs, finish, 0)

    def face(c, target):
        return remote(
            product.at[:, :, pl.ds(c * slot, slot)],
            across.at[c],
            fsend.at[c],
            frecv.at[c],
            (target, q),
        )

    face(0, first).start()

    @pl.when(has_second)
    def _():
        face(1, second).start()

    @pl.when(jnp.logical_not(has_second))
    def _():
        across[1] = jnp.zeros(across.shape[1:], jnp.float32)

    total = jnp.zeros((loads, interface), jnp.float32)
    for s in range(subs):
        total = total + search[s] * product[s]
        for c in range(2, 6):
            at = pl.ds(c * slot, slot)
            other = int(lookup[c - 2][s])
            image[s, :, at] = usable[s, :, at] * (product[s, :, at] - product[other, :, at])
    curve[...] = jnp.broadcast_to(jnp.sum(total, axis=1, keepdims=True), curve.shape)

    def drain(s, carry):
        to_twin(s, q).wait_send()
        to_far(s, q).wait_send()
        relay(s, far, far).wait_send()
        for j in range(3):
            give(s, j).wait_send()
        return carry

    lax.fori_loop(0, subs, drain, 0)
    face(0, first).wait()

    @pl.when(has_second)
    def _():
        face(1, second).wait()

    for c in range(2):
        at = pl.ds(c * slot, slot)
        for s in range(subs):
            image[s, :, at] = usable[s, :, at] * (product[s, :, at] - across[c, s])


def project_kernel(nsub, v, extra, modes, solver, basis, lifted, total, msg, gat, send, recv):
    subs, loads, _ = v.shape
    me = lax.axis_index("sub")
    q = lax.axis_index("crs")
    barrier = pltpu.get_barrier_semaphore()
    for k in range(1, nsub):
        pl.semaphore_signal(
            barrier, inc=1, device_id=((me + k) % nsub, q), device_id_type=MESH
        )
    msg[...] = extra[...]
    for s in range(subs):
        msg[:, 8 * s : 8 * s + 8] = across_rows(v[s], modes[s], PRECISE)
    pl.semaphore_wait(barrier, nsub - 1)

    def copy(k, block):
        return pltpu.make_async_remote_copy(
            src_ref=msg,
            dst_ref=gat.at[block],
            send_sem=send.at[k],
            recv_sem=recv.at[k],
            device_id=((me + k) % nsub, q),
            device_id_type=MESH,
        )

    for k in range(1, nsub):
        copy(k, me).start()
    gat[me] = msg[...]
    for k in range(1, nsub):
        copy(k, (me + nsub - k) % nsub).wait_recv()
    for k in range(1, nsub):
        copy(k, me).wait_send()
    pieces = [gat[t] for t in range(nsub)]
    total[...] = functools.reduce(lambda a, b: a + b, pieces)
    values = jnp.concatenate([piece[:, : 8 * subs] for piece in pieces], axis=1)
    y = across_rows(values, solver[...], PRECISE)
    for s in range(subs):
        lifted[s] = jnp.dot(
            y[:, 64 * s : 64 * s + 64],
            basis[s],
            precision=PRECISE,
            preferred_element_type=jnp.float32,
        )


def by_kernels(schur_block, rigid_modes, coarse_inverse, dual_rhs, stiff_diag, face_length):
    loads, subs, interface = dual_rhs.shape
    rows = schur_block.shape[1]
    slot = interface // 6
    modes = rigid_modes.shape[1]
    nsub = lax.axis_size("sub")
    sub_index = lax.axis_index("sub")
    even = sub_index % 2 == 0
    lookup = local_lookup()
    positions = jnp.arange(interface) % slot
    usable = (jnp.repeat(face_length, slot, axis=1) > positions[None, :]).astype(jnp.float32)
    up = [(i, i + 1) for i in range(nsub - 1)]
    down = [(i + 1, i) for i in range(nsub - 1)]
    f32 = jnp.float32

    def partner(vector):
        first = vector[..., :slot]
        second = vector[..., slot : 2 * slot]
        from_left = lax.ppermute(jnp.where(even, first, second), "sub", up)
        from_right = lax.ppermute(jnp.where(even, second, first), "sub", down)
        pieces = [jnp.where(even, from_right, from_left), jnp.where(even, from_left, from_right)]
        for colour in range(2, 6):
            window = vector[..., colour * slot : (colour + 1) * slot]
            pieces.append(
                jnp.concatenate([window[t : t + 1] for t in lookup[colour - 2]], axis=0)
            )
        return jnp.concatenate(pieces, axis=-1)

    rhs = jnp.swapaxes(dual_rhs, 0, 1)
    wide = jnp.pad(rigid_modes, ((0, 0), (0, 8 - modes), (0, 0)))
    marked = jnp.concatenate([wide[:, :modes], stiff_diag[:, None], wide[:, modes + 1 :]], axis=1)
    together = jnp.concatenate([rhs, marked], axis=1)
    across = partner(together)
    mask = usable[:, None, :]
    residual = mask * (rhs - across[:, :loads])
    precond = mask * (stiff_diag[:, None] + across[:, loads + modes : loads + modes + 1])

    inverse = lax.all_gather(coarse_inverse, "crs", axis=0, tiled=True)
    count = nsub * subs
    table = jnp.pad(
        inverse.reshape(nsub, subs, modes, count, modes),
        ((1, 1), (0, 0), (0, 8 - modes), (0, 0), (0, 8 - modes)),
    ).reshape(nsub + 2, subs, 8, count * 8)
    near = lax.dynamic_slice_in_dim(table, sub_index, 3, axis=0)
    before, mine, after = near[0], near[1], near[2]
    picks = [mine, jnp.where(even, after, before), jnp.where(even, before, after)]
    for colour in range(2, 6):
        picks.append(jnp.stack([mine[t] for t in lookup[colour - 2]]))
    picks.append(jnp.zeros_like(mine))
    solver = jnp.stack(picks, axis=1).reshape(subs * 64, count * 8)

    other = jnp.pad(-mask * across[:, loads : loads + modes], ((0, 0), (0, 8 - modes), (0, 0)))
    slots = jnp.asarray(np.repeat(np.eye(6, dtype=np.float32), slot, axis=1))
    spread = (other[:, None] * slots[None, :, None, :]).reshape(subs, 48, interface)
    basis = jnp.concatenate([wide * mask, spread, jnp.zeros((subs, 8, interface), f32)], axis=1)

    vector = jax.ShapeDtypeStruct((subs, loads, interface), f32)
    small = jax.ShapeDtypeStruct((loads, 128), f32)
    vmem = pl.BlockSpec(memory_space=pltpu.VMEM)
    anywhere = pl.BlockSpec(memory_space=pl.ANY)
    dma = pltpu.SemaphoreType.DMA

    def operate(search):
        return pl.pallas_call(
            functools.partial(operate_kernel, nsub, lookup),
            out_shape=(vector, small),
            in_specs=[anywhere, vmem, vmem],
            out_specs=(vmem, vmem),
            scratch_shapes=[
                pltpu.VMEM((subs, rows, interface), f32),
                pltpu.VMEM((subs, 4, loads, interface), f32),
                pltpu.VMEM((subs, 4, loads, rows), f32),
                pltpu.VMEM((subs, loads, interface), f32),
                pltpu.VMEM((2, subs, loads, slot), f32),
                dma((subs,)),
                dma((3, subs)),
                dma((3, subs)),
                dma((3, subs)),
                dma((3, subs)),
                dma((subs,)),
                dma((2,)),
                dma((2,)),
            ],
            compiler_params=pltpu.CompilerParams(
                collective_id=0, has_side_effects=True, vmem_limit_bytes=48 * 1024 * 1024
            ),
            name="operate",
        )(schur_block, search, mask)

    def lift(v, extra):
        out, total = pl.pallas_call(
            functools.partial(project_kernel, nsub),
            out_shape=(vector, small),
            in_specs=[vmem] * 5,
            out_specs=(vmem, vmem),
            scratch_shapes=[
                pltpu.VMEM((loads, 128), f32),
                pltpu.VMEM((nsub, loads, 128), f32),
                dma((nsub,)),
                dma((nsub,)),
            ],
            compiler_params=pltpu.CompilerParams(
                collective_id=1, has_side_effects=True, vmem_limit_bytes=32 * 1024 * 1024
            ),
            name="lift",
        )(v, extra, wide, solver, basis)
        return out, total[:, 64:65]

    def dots(a, b):
        return jnp.broadcast_to(jnp.sum(a * b, axis=(0, 2))[:, None], (loads, 128))

    lifted, _ = lift(residual, jnp.zeros((loads, 128), f32))
    projected = residual - lifted
    scaled = precond * projected
    lifted, energy = lift(scaled, 0.5 * dots(projected, scaled))
    search = scaled - lifted
    multipliers = None
    for iteration in range(ITERS):
        image, curve = operate(search)
        lifted, curve = lift(image, curve)
        step = energy / curve
        moved = step[None] * search
        multipliers = moved if multipliers is None else multipliers + moved
        projected = projected - step[None] * (image - lifted)
        if iteration + 1 < ITERS:
            scaled = precond * projected
            lifted, energy_new = lift(scaled, 0.5 * dots(projected, scaled))
            search = scaled - lifted + (energy_new / energy)[None] * search
            energy = energy_new
    return (jnp.swapaxes(multipliers, 0, 1), jnp.swapaxes(projected, 0, 1))


def shards(schur_block, rigid_modes, coarse_inverse, dual_rhs, stiff_diag, face_length):
    fits = dual_rhs.shape[0] == 8 and lax.axis_size("crs") == 4 and lax.axis_size("sub") <= 8
    build = by_kernels if fits else by_collectives
    return build(schur_block, rigid_modes, coarse_inverse, dual_rhs, stiff_diag, face_length)


def solution(mesh):
    return jax.shard_map(
        shards,
        mesh=mesh,
        in_specs=(
            P("sub", "crs", None),
            P("sub", None, None),
            P("crs", None),
            P("crs", "sub", None),
            P("sub", None),
            P("sub", None),
        ),
        out_specs=(P("crs", "sub", None), P("crs", "sub", None)),
        check_vma=False,
    )
```

profile of v0, /device:TPU:0, one launch (start us, length us, event | category | flops | bytes accessed | tf_op | source)
XLA Modules:
  0.0 170.7 jit_solution(2948539489497188598)
XLA Ops:
  0.7 1.1 copy.23
  1.8 1.2 copy.35
  3.3 0.8 slice_select_fusion
  4.1 1.3 collective-permute-start
  5.4 5.5 %collective-permute-start.1 = (f32[8,16,256]{2,1,0:T(8,128)}, f32[8,16,256]{2,1,0:T(8,128)S(1)}, u32[]{:S(2)}, u32[]{:S(2)}) collective-permute-start(f32[8,16,256]{2,1,0:T(8,128)} %get-tuple-element.69), channel_id=1, source_target_pairs={{0,4},{4,8},{8,12},{12,16},{16,20},{20,24},{24,28},{1,5},{5,9},{9,... | collective-permute-start | bytes 393224 | tf_op jit(solution)/shard_map/ppermute | solution.py:445
  10.9 8.1 %all_gather.3 = f32[384,384]{1,0:T(8,128)S(1)} all-gather(f32[96,384]{1,0:T(8,128)S(1)} %copy-done.3), channel_id=1, replica_groups=mesh['sub'=8,'crs'=4] {'crs'}, dimensions={0}, use_global_device_ids=true | all-gather | bytes 737280 | tf_op jit(solution)/shard_map/all_gather | solution.py:464
  19.0 14.3 %reshape.151 = f32[8,8,6,64,6]{4,3,2,1,0:T(8,128)} reshape(f32[384,384]{1,0:T(8,128)S(1)} %all_gather.3) | data formatting | bytes 1179648 | tf_op jit(solution)/shard_map/reshape | solution.py:467
  33.3 12.6 %pad.12 = f32[10,8,8,64,8]{4,3,2,1,0:T(8,128)} pad(f32[8,8,6,64,6]{4,3,2,1,0:T(8,128)} %reshape.151, f32[]{:T(128)} %constant.45.clone.1), padding=1_1x0_0x0_2x0_0x0_2 | pad | bytes 1900548 | tf_op jit(solution)/shard_map/jit(_pad)/pad | solution.py:466
  45.9 15.4 %reshape.152 = f32[10,8,8,512]{3,2,1,0:T(8,128)S(1)} reshape(f32[10,8,8,64,8]{4,3,2,1,0:T(8,128)} %pad.12) | data formatting | bytes 2621440 | tf_op jit(solution)/shard_map/reshape | solution.py:469
  62.8 0.7 bitcast_dynamic-update-slice_fusion.5
  63.4 0.7 bitcast_dynamic-update-slice_fusion.4
  67.5 1.3 copy.25
  69.2 0.9 fusion.7
  70.2 0.9 slice_dynamic-update-slice_fusion
  71.6 0.8 copy-done.1
  73.4 9.9 %lift.5 = (f32[8,8,1536]{2,1,0:T(8,128)S(1)}, f32[8,128]{1,0:T(8,128)}) custom-call(f32[8,8,1536]{2,1,0:T(8,128)S(1)} %get-tuple-element.73.v, f32[8,128]{1,0:T(8,128)S(1)} %broadcast_in_dim.14.extra, f32[8,8,1536]{2,1,0:T(8,128)S(1)} %get-tuple-element.72.modes, f32[512,512]{1,0:T(8,128)S(1)} %bitcast.117, f32[8,64,1536]{2,1,0:T(8,128)S(1)} %maximum_maximum_fusion.basis), custom_call_target="tpu_custom_call" | custom-call | tf_op jit(solution)/shard_map/lift/pallas_call | solution.py:517
  83.8 8.8 %lift.6 = (f32[8,8,1536]{2,1,0:T(8,128)S(1)}, f32[8,128]{1,0:T(8,128)S(1)}) custom-call(f32[8,8,1536]{2,1,0:T(8,128)S(1)} %broadcast_multiply_fusion.2.v, f32[8,128]{1,0:T(8,128)S(1)} %broadcast_in_dim.16.extra, f32[8,8,1536]{2,1,0:T(8,128)S(1)} %get-tuple-element.72.modes, f32[512,512]{1,0:T(8,128)S(1)} %bitcast.118, ...), custom_call_target="tpu_custom_call" | custom-call | tf_op jit(solution)/shard_map/lift/pallas_call | solution.py:517
  92.7 22.8 %operate.2 = (f32[8,8,1536]{2,1,0:T(8,128)S(1)}, f32[8,128]{1,0:T(8,128)S(1)}) custom-call(f32[8,384,1536]{2,1,0:T(8,128)} %schur.3, f32[8,8,1536]{2,1,0:T(8,128)S(1)} %fusion.2.search, f32[8,1,1536]{2,1,0:T(1,128)S(1)} %compare_convert_fusion.usable), custom_call_target="tpu_custom_call" | custom-call | tf_op jit(solution)/shard_map/operate/pallas_call | solution.py:490
  115.5 10.1 %lift.7 = (f32[8,8,1536]{2,1,0:T(8,128)S(1)}, f32[8,128]{1,0:T(8,128)S(1)}) custom-call(f32[8,8,1536]{2,1,0:T(8,128)S(1)} %get-tuple-element.18.v, f32[8,128]{1,0:T(8,128)S(1)} %get-tuple-element.19.extra, f32[8,8,1536]{2,1,0:T(8,128)S(1)} %get-tuple-element.72.modes, f32[512,512]{1,0:T(8,128)S(1)} %bitcast.119, f32[8,64,1536]{2,1,0:T(8,128)S(1)} %maximum_maximum_fusion.basis), custom_call_target="tpu_custom_call" | custom-call | tf_op jit(solution)/shard_map/lift/pallas_call | solution.py:517
  126.2 8.8 %lift.8 = (f32[8,8,1536]{2,1,0:T(8,128)S(1)}, f32[8,128]{1,0:T(8,128)S(1)}) custom-call(f32[8,8,1536]{2,1,0:T(8,128)S(1)} %broadcast_multiply_fusion.1.v, f32[8,128]{1,0:T(8,128)S(1)} %broadcast_in_dim.17.extra, f32[8,8,1536]{2,1,0:T(8,128)S(1)} %get-tuple-element.72.modes, f32[512,512]{1,0:T(8,128)S(1)} %bitcast.120, ...), custom_call_target="tpu_custom_call" | custom-call | tf_op jit(solution)/shard_map/lift/pallas_call | solution.py:517
  135.4 22.6 %operate.3 = (f32[8,8,1536]{2,1,0:T(8,128)S(1)}, f32[8,128]{1,0:T(8,128)S(1)}) custom-call(f32[8,384,1536]{2,1,0:T(8,128)} %schur.3, f32[8,8,1536]{2,1,0:T(8,128)S(1)} %multiply_add_fusion.search, f32[8,1,1536]{2,1,0:T(1,128)S(1)} %compare_convert_fusion.usable), custom_call_target="tpu_custom_call" | custom-call | tf_op jit(solution)/shard_map/operate/pallas_call | solution.py:490
  158.0 10.3 %lift.9 = (f32[8,8,1536]{2,1,0:T(8,128)S(1)}, f32[8,128]{1,0:T(8,128)S(1)}) custom-call(f32[8,8,1536]{2,1,0:T(8,128)S(1)} %get-tuple-element.24.v, f32[8,128]{1,0:T(8,128)S(1)} %get-tuple-element.25.extra, f32[8,8,1536]{2,1,0:T(8,128)S(1)} %get-tuple-element.72.modes, f32[512,512]{1,0:T(8,128)S(1)} %bitcast.121, f32[8,64,1536]{2,1,0:T(8,128)S(1)} %maximum_maximum_fusion.basis), custom_call_target="tpu_custom_call" | custom-call | tf_op jit(solution)/shard_map/lift/pallas_call | solution.py:517
  168.7 1.0 copy.26
  169.7 1.0 copy.27
  (87 shorter events, 8.6 us)
Async XLA Ops:
  0.6 2.4 %copy-start.2 = (f32[8,1536]{1,0:T(8,128)S(1)}, f32[8,1536]{1,0:T(8,128)}, u32[]{:S(2)}) copy-start(f32[8,1536]{1,0:T(8,128)} %param.11) | copy-start | bytes 147460
  3.0 7.9 %copy-start.3 = (f32[96,384]{1,0:T(8,128)S(1)}, f32[96,384]{1,0:T(8,128)}, u32[]{:S(2)}) copy-start(f32[96,384]{1,0:T(8,128)} %param.9) | copy-start | bytes 442372
  3.3 7.6 %copy-start = (f32[8,16,1536]{2,1,0:T(8,128)}, f32[8,16,1536]{2,1,0:T(8,128)S(1)}, u32[]{:S(2)}) copy-start(f32[8,16,1536]{2,1,0:T(8,128)S(1)} %pad_maximum_fusion) | copy-start | bytes 2359300
  4.1 66.0 %collective-permute-start = (f32[8,16,256]{2,1,0:T(8,128)}, f32[8,16,256]{2,1,0:T(8,128)S(1)}, u32[]{:S(2)}, u32[]{:S(2)}) collective-permute-start(f32[8,16,256]{2,1,0:T(8,128)} %get-tuple-element.70), channel_id=1, source_target_pairs={{4,0},{8,4},{12,8},{16,12},{20,16},{24,20},{28,24},{5,1},{9,5},{13... | collective-permute-start | bytes 393224 | tf_op jit(solution)/shard_map/ppermute | solution.py:446
  5.4 64.7 %collective-permute-start.1 = (f32[8,16,256]{2,1,0:T(8,128)}, f32[8,16,256]{2,1,0:T(8,128)S(1)}, u32[]{:S(2)}, u32[]{:S(2)}) collective-permute-start(f32[8,16,256]{2,1,0:T(8,128)} %get-tuple-element.69), channel_id=1, source_target_pairs={{0,4},{4,8},{8,12},{12,16},{16,20},{20,24},{24,28},{1,5},{5,9},{9,... | collective-permute-start | bytes 393224 | tf_op jit(solution)/shard_map/ppermute | solution.py:445
  66.2 2.6 %copy-start.6 = (s32[8,6]{1,0:T(8,128)S(1)}, s32[8,6]{1,0:T(8,128)}, u32[]{:S(2)}) copy-start(s32[8,6]{1,0:T(8,128)} %param.12) | copy-start | bytes 580
  66.2 2.7 %copy-start.5 = (f32[6,1536]{1,0:T(8,128)S(1)}, f32[6,1536]{1,0:T(8,128)}, u32[]{:S(2)}) copy-start(f32[6,1536]{1,0:T(8,128)} %constant.48.clone) | copy-start | bytes 110596
  66.9 2.2 %copy-start.4 = (s32[1536]{0:T(1024)S(1)}, s32[1536]{0:T(1024)}, u32[]{:S(2)}) copy-start(s32[1536]{0:T(1024)} %add_select_fusion) | copy-start | bytes 18436
  71.4 1.0 copy-start.1
where the time goes:
time: 171 us
  Pallas kernels  93.4 us (55%)
  local copies, waits for them, and re-layouts  55.2 us (32%)
  blocking collectives  8.08 us (5%)
  starting transfers between devices  6.79 us (4%)
  other arithmetic  6.07 us (4%)
    pallas_call x5, Pallas kernels, lift(): pl.pallas_call(functools.partial(project_kernel, nsub), out_shape=(vector...  47.9 us
    pallas_call x2, Pallas kernels, operate(): pl.pallas_call(functools.partial(operate_kernel, nsub, lookup), out_shape...  45.5 us
    reshape x1, local copies, waits for them, and re-layouts, by_kernels(): table = jnp.pad(inverse.reshape(nsub, subs, modes, count, modes), ((1, 1)...  15.4 us
    reshape x1, local copies, waits for them, and re-layouts, by_kernels(): inverse.reshape(nsub, subs, modes, count, modes)  14.3 us
    pad x1, local copies, waits for them, and re-layouts, by_kernels(): jnp.pad(inverse.reshape(nsub, subs, modes, count, modes), ((1, 1), (0, 0)...  12.6 us
    unnamed x39, local copies, waits for them, and re-layouts  9.62 us
    all_gather x1, blocking collectives, by_kernels(): inverse = lax.all_gather(coarse_inverse, 'crs', axis=0, tiled=True)  8.08 us
    ppermute x1, starting transfers between devices, partner(): from_left = lax.ppermute(jnp.where(even, first, second), 'sub', up)  5.51 us
  transfers between devices with their start and end apart: 2, of which 0 were waited for; matrix products, arithmetic and copies ran while one was open for 30% of the time, Pallas kernels for 0%

commit v1 on v0

--- a/solution.py
+++ b/solution.py
@@ -424,6 +424,88 @@
         )
 
 
+def begin_kernel(nsub, edges, block, across, inverse, fsend, frecv, gsend, grecv, osem):
+    me = lax.axis_index("sub")
+    q = lax.axis_index("crs")
+    core = q % 2
+    twin = q + 1 - 2 * core
+    far = (q + 2) % 4
+    diagonal = (twin + 2) % 4
+    odd = me % 2
+    first = me + 1 - 2 * odd
+    second = me - 1 + 2 * odd
+    has_second = jnp.logical_and(second >= 0, second < nsub)
+    slot = across.shape[3]
+    barrier = pltpu.get_barrier_semaphore()
+    for peer in (twin, far):
+        pl.semaphore_signal(barrier, inc=1, device_id=(me, peer), device_id_type=MESH)
+    pl.semaphore_signal(barrier, inc=1, device_id=(first, q), device_id_type=MESH)
+
+    @pl.when(has_second)
+    def _():
+        pl.semaphore_signal(barrier, inc=1, device_id=(second, q), device_id_type=MESH)
+
+    pl.semaphore_wait(barrier, jnp.where(has_second, 4, 3))
+
+    def remote(src, dst, send, recv, target):
+        return pltpu.make_async_remote_copy(
+            src_ref=src,
+            dst_ref=dst,
+            send_sem=send,
+            recv_sem=recv,
+            device_id=target,
+            device_id_type=MESH,
+        )
+
+    def to_far(at):
+        return remote(block, inverse.at[at], gsend.at[1], grecv.at[1], (me, far))
+
+    def to_twin(at):
+        return remote(block, inverse.at[at], gsend.at[0], grecv.at[0], (me, twin))
+
+    def relay(at):
+        return remote(inverse.at[far], inverse.at[at], gsend.at[2], grecv.at[2], (me, twin))
+
+    def face(c, target):
+        return remote(
+            edges.at[:, :, pl.ds(c * slot, slot)],
+            across.at[c],
+            fsend.at[c],
+            frecv.at[c],
+            (target, q),
+        )
+
+    keep = pltpu.make_async_copy(block, inverse.at[q], osem)
+    to_far(q).start()
+    to_twin(q).start()
+    face(0, first).start()
+
+    @pl.when(has_second)
+    def _():
+        face(1, second).start()
+
+    keep.start()
+
+    @pl.when(jnp.logical_not(has_second))
+    def _():
+        across[1] = jnp.zeros(across.shape[1:], jnp.float32)
+
+    to_far(far).wait_recv()
+    relay(far).start()
+    keep.wait()
+    to_twin(twin).wait_recv()
+    to_far(q).wait_send()
+    to_twin(q).wait_send()
+    face(0, first).wait()
+
+    @pl.when(has_second)
+    def _():
+        face(1, second).wait()
+
+    relay(diagonal).wait_recv()
+    relay(far).wait_send()
+
+
 def by_kernels(schur_block, rigid_modes, coarse_inverse, dual_rhs, stiff_diag, face_length):
     loads, subs, interface = dual_rhs.shape
     rows = schur_block.shape[1]
@@ -435,45 +517,59 @@
     lookup = local_lookup()
     positions = jnp.arange(interface) % slot
     usable = (jnp.repeat(face_length, slot, axis=1) > positions[None, :]).astype(jnp.float32)
-    up = [(i, i + 1) for i in range(nsub - 1)]
-    down = [(i + 1, i) for i in range(nsub - 1)]
     f32 = jnp.float32
 
-    def partner(vector):
-        first = vector[..., :slot]
-        second = vector[..., slot : 2 * slot]
-        from_left = lax.ppermute(jnp.where(even, first, second), "sub", up)
-        from_right = lax.ppermute(jnp.where(even, second, first), "sub", down)
-        pieces = [jnp.where(even, from_right, from_left), jnp.where(even, from_left, from_right)]
-        for colour in range(2, 6):
-            window = vector[..., colour * slot : (colour + 1) * slot]
-            pieces.append(
-                jnp.concatenate([window[t : t + 1] for t in lookup[colour - 2]], axis=0)
-            )
-        return jnp.concatenate(pieces, axis=-1)
+    vmem = pl.BlockSpec(memory_space=pltpu.VMEM)
+    anywhere = pl.BlockSpec(memory_space=pl.ANY)
+    dma = pltpu.SemaphoreType.DMA
 
     rhs = jnp.swapaxes(dual_rhs, 0, 1)
     wide = jnp.pad(rigid_modes, ((0, 0), (0, 8 - modes), (0, 0)))
     marked = jnp.concatenate([wide[:, :modes], stiff_diag[:, None], wide[:, modes + 1 :]], axis=1)
     together = jnp.concatenate([rhs, marked], axis=1)
-    across = partner(together)
+    edges, inverse = pl.pallas_call(
+        functools.partial(begin_kernel, nsub),
+        out_shape=(
+            jax.ShapeDtypeStruct((2, subs, together.shape[1], slot), f32),
+            jax.ShapeDtypeStruct((4,) + coarse_inverse.shape, f32),
+        ),
+        in_specs=[vmem, vmem],
+        out_specs=(vmem, vmem),
+        scratch_shapes=[dma((2,)), dma((2,)), dma((3,)), dma((3,)), dma],
+        compiler_params=pltpu.CompilerParams(
+            collective_id=2, has_side_effects=True, vmem_limit_bytes=16 * 1024 * 1024
+        ),
+        name="begin",
+    )(together[:, :, : 2 * slot], coarse_inverse)
+    pieces = [edges[0], edges[1]]
+    for colour in range(2, 6):
+        window = together[:, :, colour * slot : (colour + 1) * slot]
+        pieces.append(jnp.concatenate([window[t : t + 1] for t in lookup[colour - 2]], axis=0))
+    across = jnp.concatenate(pieces, axis=-1)
     mask = usable[:, None, :]
     residual = mask * (rhs - across[:, :loads])
     precond = mask * (stiff_diag[:, None] + across[:, loads + modes : loads + modes + 1])
 
-    inverse = lax.all_gather(coarse_inverse, "crs", axis=0, tiled=True)
-    count = nsub * subs
-    table = jnp.pad(
-        inverse.reshape(nsub, subs, modes, count, modes),
-        ((1, 1), (0, 0), (0, 8 - modes), (0, 0), (0, 8 - modes)),
-    ).reshape(nsub + 2, subs, 8, count * 8)
-    near = lax.dynamic_slice_in_dim(table, sub_index, 3, axis=0)
-    before, mine, after = near[0], near[1], near[2]
-    picks = [mine, jnp.where(even, after, before), jnp.where(even, before, after)]
-    for colour in range(2, 6):
-        picks.append(jnp.stack([mine[t] for t in lookup[colour - 2]]))
-    picks.append(jnp.zeros_like(mine))
-    solver = jnp.stack(picks, axis=1).reshape(subs * 64, count * 8)
+    own = subs * modes
+    order = nsub * own
+    inverse = jnp.pad(inverse.reshape(order, order), ((own, own), (0, 0)))
+    near = lax.dynamic_slice_in_dim(inverse, sub_index * own, 3 * own, axis=0)
+    before, mine, after = near[:own], near[own : 2 * own], near[2 * own :]
+    near = jnp.concatenate(
+        [mine, jnp.where(even, after, before), jnp.where(even, before, after)], axis=0
+    )
+    widen = np.zeros((order, nsub * subs * 8), np.float32)
+    for at in range(order):
+        widen[at, at // modes * 8 + at % modes] = 1.0
+    choose = np.zeros((subs, 8, 8, 3, subs, modes), np.float32)
+    for s in range(subs):
+        sources = [(0, s), (1, s), (2, s)] + [(0, int(lookup[c][s])) for c in range(4)]
+        for j, (group, t) in enumerate(sources):
+            for m in range(modes):
+                choose[s, j, m, group, t, m] = 1.0
+    choose = choose.reshape(subs * 64, 3 * own)
+    solver = jnp.dot(near, jnp.asarray(widen), precision=PRECISE)
+    solver = jnp.dot(jnp.asarray(choose), solver, precision=PRECISE)
 
     other = jnp.pad(-mask * across[:, loads : loads + modes], ((0, 0), (0, 8 - modes), (0, 0)))
     slots = jnp.asarray(np.repeat(np.eye(6, dtype=np.float32), slot, axis=1))
@@ -482,9 +578,6 @@
 
     vector = jax.ShapeDtypeStruct((subs, loads, interface), f32)
     small = jax.ShapeDtypeStruct((loads, 128), f32)
-    vmem = pl.BlockSpec(memory_space=pltpu.VMEM)
-    anywhere = pl.BlockSpec(memory_space=pl.ANY)
-    dma = pltpu.SemaphoreType.DMA
 
     def operate(search):
         return pl.pallas_call(

time: 171 us -> 118 us (0.69)
  local copies, waits for them, and re-layouts: 55.2 us -> 8.03 us
  Pallas kernels: 93.4 us -> 104 us
  blocking collectives: 8.08 us -> 0 us
  starting transfers between devices: 6.79 us -> 0 us
  other arithmetic: 6.07 us -> 3.29 us
    reshape x2 -> x0, local copies, waits for them, and re-layouts: 29.7 us -> none  [the longest x1 15.4 us: by_kernels(): table = jnp.pad(inverse.reshape(nsub, subs, modes, count, modes), ((1, 1)...]
    pad x1 -> x0, local copies, waits for them, and re-layouts: 12.6 us -> none  [by_kernels(): jnp.pad(inverse.reshape(nsub, subs, modes, count, modes), ((1, 1), (0, 0)...]
    pallas_call x0 -> x1, Pallas kernels: none -> 9.21 us  [by_kernels(): pl.pallas_call(functools.partial(begin_kernel, nsub), out_shape=(jax.Shap...]
    all_gather x1 -> x0, blocking collectives: 8.08 us -> none  [by_kernels(): inverse = lax.all_gather(coarse_inverse, 'crs', axis=0, tiled=True)]
    ppermute x2 -> x0, starting transfers between devices: 6.79 us -> none  [the longest x1 5.51 us: partner(): from_left = lax.ppermute(jnp.where(even, first, second), 'sub', up)]
    unnamed x39 -> x19, local copies, waits for them, and re-layouts: 9.62 us -> 5.99 us
    another operation x4 -> x0, local copies, waits for them, and re-layouts: 1.99 us -> none  [the longest x2 1.96 us: by_kernels(): solver = jnp.stack(picks, axis=1).reshape(subs * 64, count * 8)]
  transfers between devices with their start and end apart: 2 -> 0, of which waited for: 0 -> 0; matrix products, arithmetic and copies ran while one was open for 30% -> 0% of each run, Pallas kernels for 0% -> 0%
where the time goes in v1:
time: 118 us
  Pallas kernels  104 us (88%)
  local copies, waits for them, and re-layouts  8.03 us (7%)
  other arithmetic  3.29 us (3%)
  matrix products  1.67 us (1%)
    pallas_call x5, Pallas kernels, lift(): pl.pallas_call(functools.partial(project_kernel, nsub), out_shape=(vector...  49.2 us
    pallas_call x2, Pallas kernels, operate(): pl.pallas_call(functools.partial(operate_kernel, nsub, lookup), out_shape...  45.7 us
    pallas_call x1, Pallas kernels, by_kernels(): pl.pallas_call(functools.partial(begin_kernel, nsub), out_shape=(jax.Shap...  9.21 us
    unnamed x19, local copies, waits for them, and re-layouts  5.99 us

profile of v1, /device:TPU:0, one launch (start us, length us, event | category | flops | bytes accessed | tf_op | source)
XLA Modules:
  0.0 118.1 jit_solution(2278548621082851807)
XLA Ops:
  0.8 0.8 copy.16
  1.7 0.8 broadcast_in_dim.13
  2.6 0.8 broadcast_bitcast_fusion
  3.4 1.2 %copy.19 = f32[8,6,1536]{2,1,0:T(8,128)S(1)} copy(f32[8,6,1536]{2,0,1:T(8,128)} %param.10) | data formatting | bytes 589824 | tf_op args[1]
  4.6 1.2 %copy.30 = f32[8,8,1536]{2,0,1:T(8,128)S(1)} copy(f32[8,8,1536]{2,1,0:T(8,128)} %param.12) | data formatting | bytes 786432 | tf_op args[3]
  6.1 9.2 %begin.1 = (f32[2,8,16,256]{3,2,1,0:T(8,128)S(1)}, f32[4,96,384]{2,1,0:T(8,128)S(1)}) custom-call(f32[8,16,512]{2,1,0:T(8,128)S(1)} %slice.183.edges, f32[96,384]{1,0:T(8,128)S(1)} %copy-done), custom_call_target="tpu_custom_call" | custom-call | tf_op jit(solution)/shard_map/begin/pallas_call | solution.py:530
  15.4 0.7 fusion.1
  16.1 1.0 fusion.14.solver
  17.5 0.6 copy-done.4
  18.3 0.3 broadcast_multiply_fusion
  18.7 0.3 bitcast_multiply_fusion
  19.0 0.4 maximum_maximum_fusion.basis
  19.4 10.7 %lift.5 = (f32[8,8,1536]{2,1,0:T(8,128)S(1)}, f32[8,128]{1,0:T(8,128)}) custom-call(f32[8,8,1536]{2,1,0:T(8,128)S(1)} %get-tuple-element.49.v, f32[8,128]{1,0:T(8,128)S(1)} %broadcast_in_dim.14.extra, f32[8,8,1536]{2,1,0:T(8,128)S(1)} %get-tuple-element.48.modes, f32[512,512]{1,0:T(8,128)S(1)} %fusion.14.solver, f32[8,64,1536]{2,1,0:T(8,128)S(1)} %maximum_maximum_fusion.basis), custom_call_target="tpu_custom_call" | custom-call | tf_op jit(solution)/shard_map/lift/pallas_call | solution.py:610
  30.1 0.2 multiply_reduce_fusion.1
  30.5 9.0 %lift.6 = (f32[8,8,1536]{2,1,0:T(8,128)S(1)}, f32[8,128]{1,0:T(8,128)S(1)}) custom-call(f32[8,8,1536]{2,1,0:T(8,128)S(1)} %broadcast_multiply_fusion.2.v, f32[8,128]{1,0:T(8,128)S(1)} %broadcast_in_dim.16.extra, f32[8,8,1536]{2,1,0:T(8,128)S(1)} %get-tuple-element.48.modes, f32[512,512]{1,0:T(8,128)S(1)} %fusion.14.solver, ...), custom_call_target="tpu_custom_call" | custom-call | tf_op jit(solution)/shard_map/lift/pallas_call | solution.py:610
  39.6 23.1 %operate.2 = (f32[8,8,1536]{2,1,0:T(8,128)S(1)}, f32[8,128]{1,0:T(8,128)S(1)}) custom-call(f32[8,384,1536]{2,1,0:T(8,128)} %schur.3, f32[8,8,1536]{2,1,0:T(8,128)S(1)} %fusion.7.search, f32[8,1,1536]{2,1,0:T(1,128)S(1)} %compare_convert_fusion.usable), custom_call_target="tpu_custom_call" | custom-call | tf_op jit(solution)/shard_map/operate/pallas_call | solution.py:583
  62.7 10.3 %lift.7 = (f32[8,8,1536]{2,1,0:T(8,128)S(1)}, f32[8,128]{1,0:T(8,128)S(1)}) custom-call(f32[8,8,1536]{2,1,0:T(8,128)S(1)} %get-tuple-element.22.v, f32[8,128]{1,0:T(8,128)S(1)} %get-tuple-element.23.extra, f32[8,8,1536]{2,1,0:T(8,128)S(1)} %get-tuple-element.48.modes, f32[512,512]{1,0:T(8,128)S(1)} %fusion.14.solver, ...), custom_call_target="tpu_custom_call" | custom-call | tf_op jit(solution)/shard_map/lift/pallas_call | solution.py:610
  73.2 0.3 multiply_reduce_fusion
  73.6 8.9 %lift.8 = (f32[8,8,1536]{2,1,0:T(8,128)S(1)}, f32[8,128]{1,0:T(8,128)S(1)}) custom-call(f32[8,8,1536]{2,1,0:T(8,128)S(1)} %broadcast_multiply_fusion.1.v, f32[8,128]{1,0:T(8,128)S(1)} %broadcast_in_dim.17.extra, f32[8,8,1536]{2,1,0:T(8,128)S(1)} %get-tuple-element.48.modes, f32[512,512]{1,0:T(8,128)S(1)} %fusion.14.solver, ...), custom_call_target="tpu_custom_call" | custom-call | tf_op jit(solution)/shard_map/lift/pallas_call | solution.py:610
  82.9 22.6 %operate.3 = (f32[8,8,1536]{2,1,0:T(8,128)S(1)}, f32[8,128]{1,0:T(8,128)S(1)}) custom-call(f32[8,384,1536]{2,1,0:T(8,128)} %schur.3, f32[8,8,1536]{2,1,0:T(8,128)S(1)} %multiply_add_fusion.search, f32[8,1,1536]{2,1,0:T(1,128)S(1)} %compare_convert_fusion.usable), custom_call_target="tpu_custom_call" | custom-call | tf_op jit(solution)/shard_map/operate/pallas_call | solution.py:583
  105.4 10.3 %lift.9 = (f32[8,8,1536]{2,1,0:T(8,128)S(1)}, f32[8,128]{1,0:T(8,128)S(1)}) custom-call(f32[8,8,1536]{2,1,0:T(8,128)S(1)} %get-tuple-element.28.v, f32[8,128]{1,0:T(8,128)S(1)} %get-tuple-element.29.extra, f32[8,8,1536]{2,1,0:T(8,128)S(1)} %get-tuple-element.48.modes, f32[512,512]{1,0:T(8,128)S(1)} %fusion.14.solver, ...), custom_call_target="tpu_custom_call" | custom-call | tf_op jit(solution)/shard_map/lift/pallas_call | solution.py:610
  115.9 0.2 subtract_bitcast_fusion
  116.2 1.0 copy.22
  117.1 1.0 copy.21
  (55 shorter events, 2.0 us)
Async XLA Ops:
  0.6 14.8 %copy-start.2 = (f32[384,512]{1,0:T(8,128)S(1)}, f32[384,512]{1,0:T(8,128)}, u32[]{:S(2)}) copy-start(f32[384,512]{1,0:T(8,128)} %constant.53.clone) | copy-start | bytes 2359300
  0.6 5.5 %copy-start = (f32[96,384]{1,0:T(8,128)S(1)}, f32[96,384]{1,0:T(8,128)}, u32[]{:S(2)}) copy-start(f32[96,384]{1,0:T(8,128)} %block.1) | copy-start | bytes 442372
  3.4 12.7 %copy-start.3 = (f32[512,144]{1,0:T(8,128)S(1)}, f32[512,144]{1,0:T(8,128)}, u32[]{:S(2)}) copy-start(f32[512,144]{1,0:T(8,128)} %constant.54.clone) | copy-start | bytes 884740
  17.3 0.8 copy-start.4
  17.3 1.0 copy-start.1

commit v2 on v1

--- a/solution.py
+++ b/solution.py
@@ -188,28 +188,12 @@
     return high, (x - high.astype(jnp.float32)).astype(jnp.bfloat16)
 
 
-def operate_kernel(
-    nsub,
-    lookup,
-    schur,
-    search,
-    usable,
-    image,
-    curve,
-    hold,
-    gath,
-    res,
-    product,
-    across,
-    load_sem,
-    gsend,
-    grecv,
-    asend,
-    arecv,
-    osem,
-    fsend,
-    frecv,
-):
+def load_copy(schur, hold, load_sem, s):
+    return pltpu.make_async_copy(schur.at[s], hold.at[s], load_sem.at[s])
+
+
+def operate(nsub, lookup, repeated, load, search, usable, image, hold, res, buffers):
+    gath, product, across, gsend, grecv, asend, arecv, osem, fsend, frecv = buffers
     subs, loads, interface = search.shape
     rows = hold.shape[1]
     slot = interface // 6
@@ -224,25 +208,6 @@
     second = me - 1 + 2 * odd
     has_second = jnp.logical_and(second >= 0, second < nsub)
 
-    def load(s):
-        return pltpu.make_async_copy(schur.at[s], hold.at[s], load_sem.at[s])
-
-    def start_load(s, carry):
-        load(s).start()
-        return carry
-
-    lax.fori_loop(0, subs, start_load, 0)
-    barrier = pltpu.get_barrier_semaphore()
-    for peer in (twin, far, diagonal):
-        pl.semaphore_signal(barrier, inc=1, device_id=(me, peer), device_id_type=MESH)
-    pl.semaphore_signal(barrier, inc=1, device_id=(first, q), device_id_type=MESH)
-
-    @pl.when(has_second)
-    def _():
-        pl.semaphore_signal(barrier, inc=1, device_id=(second, q), device_id_type=MESH)
-
-    pl.semaphore_wait(barrier, jnp.where(has_second, 5, 4))
-
     def remote(src, dst, send, recv, target):
         return pltpu.make_async_remote_copy(
             src_ref=src,
@@ -308,7 +273,8 @@
         def _():
             forward(s + 1)
 
-        load(s).wait()
+        if not repeated:
+            load(s).wait()
         w_high, w_low = halves(hold[s])
         to_twin(s, twin).wait_recv()
         relay(s, far, diagonal).wait_recv()
@@ -357,7 +323,7 @@
             at = pl.ds(c * slot, slot)
             other = int(lookup[c - 2][s])
             image[s, :, at] = usable[s, :, at] * (product[s, :, at] - product[other, :, at])
-    curve[...] = jnp.broadcast_to(jnp.sum(total, axis=1, keepdims=True), curve.shape)
+    curve = jnp.sum(total, axis=1, keepdims=True)
 
     def drain(s, carry):
         to_twin(s, q).wait_send()
@@ -378,21 +344,17 @@
         at = pl.ds(c * slot, slot)
         for s in range(subs):
             image[s, :, at] = usable[s, :, at] * (product[s, :, at] - across[c, s])
-
-
-def project_kernel(nsub, v, extra, modes, solver, basis, lifted, total, msg, gat, send, recv):
+    return curve
+
+
+def lift(nsub, v, extra, modes, solver, basis, lifted, msg, buffers):
+    gat, send, recv = buffers
     subs, loads, _ = v.shape
     me = lax.axis_index("sub")
     q = lax.axis_index("crs")
-    barrier = pltpu.get_barrier_semaphore()
-    for k in range(1, nsub):
-        pl.semaphore_signal(
-            barrier, inc=1, device_id=((me + k) % nsub, q), device_id_type=MESH
-        )
-    msg[...] = extra[...]
+    msg[...] = jnp.broadcast_to(extra, msg.shape)
     for s in range(subs):
         msg[:, 8 * s : 8 * s + 8] = across_rows(v[s], modes[s], PRECISE)
-    pl.semaphore_wait(barrier, nsub - 1)
 
     def copy(k, block):
         return pltpu.make_async_remote_copy(
@@ -412,7 +374,7 @@
     for k in range(1, nsub):
         copy(k, me).wait_send()
     pieces = [gat[t] for t in range(nsub)]
-    total[...] = functools.reduce(lambda a, b: a + b, pieces)
+    total = functools.reduce(lambda a, b: a + b, pieces)
     values = jnp.concatenate([piece[:, : 8 * subs] for piece in pieces], axis=1)
     y = across_rows(values, solver[...], PRECISE)
     for s in range(subs):
@@ -422,6 +384,94 @@
             precision=PRECISE,
             preferred_element_type=jnp.float32,
         )
+    return total[:, 64:65]
+
+
+def main_kernel(
+    nsub,
+    lookup,
+    schur,
+    residual,
+    precond,
+    usable,
+    modes,
+    solver,
+    basis,
+    multipliers,
+    projected,
+    hold,
+    res,
+    search,
+    work,
+    lifted,
+    msg,
+    load_sem,
+    *buffers,
+):
+    subs, loads, interface = residual.shape
+    me = lax.axis_index("sub")
+    q = lax.axis_index("crs")
+    load = functools.partial(load_copy, schur, hold, load_sem)
+
+    def start_load(s, carry):
+        load(s).start()
+        return carry
+
+    lax.fori_loop(0, subs, start_load, 0)
+    barrier = pltpu.get_barrier_semaphore()
+    for k in range(1, nsub):
+        pl.semaphore_signal(
+            barrier, inc=1, device_id=((me + k) % nsub, q), device_id_type=MESH
+        )
+    for k in range(1, 4):
+        pl.semaphore_signal(barrier, inc=1, device_id=(me, (q + k) % 4), device_id_type=MESH)
+    pl.semaphore_wait(barrier, nsub + 2)
+
+    operates = [buffers[10 * n : 10 * n + 10] for n in range(ITERS)]
+    lifts = [buffers[10 * ITERS + 3 * n : 10 * ITERS + 3 * n + 3] for n in range(2 * ITERS + 1)]
+
+    def lift_of(count, v, extra):
+        return lift(nsub, v, extra, modes, solver, basis, lifted, msg, lifts[count])
+
+    def scale():
+        total = jnp.zeros((loads, interface), jnp.float32)
+        for s in range(subs):
+            scaled = precond[s] * projected[s]
+            work[s] = scaled
+            total = total + projected[s] * scaled
+        return 0.5 * jnp.sum(total, axis=1, keepdims=True)
+
+    lift_of(0, residual, jnp.zeros((loads, 1), jnp.float32))
+    for s in range(subs):
+        projected[s] = residual[s] - lifted[s]
+    energy = lift_of(1, work, scale())
+    for s in range(subs):
+        search[s] = work[s] - lifted[s]
+    for iteration in range(ITERS):
+        curve = operate(
+            nsub,
+            lookup,
+            iteration > 0,
+            load,
+            search,
+            usable,
+            work,
+            hold,
+            res,
+            operates[iteration],
+        )
+        curve = lift_of(2 + 2 * iteration, work, curve)
+        step = energy / curve
+        for s in range(subs):
+            moved = step * search[s]
+            multipliers[s] = moved if iteration == 0 else multipliers[s] + moved
+            projected[s] = projected[s] - step * (work[s] - lifted[s])
+        if iteration + 1 < ITERS:
+            energy_new = lift_of(3 + 2 * iteration, work, scale())
+            ratio = energy_new / energy
+            for s in range(subs):
+                search[s] = work[s] - lifted[s] + ratio * search[s]
+            energy = energy_new
 
 
 def begin_kernel(nsub, edges, block, across, inverse, fsend, frecv, gsend, grecv, osem):
@@ -537,7 +587,7 @@
         out_specs=(vmem, vmem),
         scratch_shapes=[dma((2,)), dma((2,)), dma((3,)), dma((3,)), dma],
         compiler_params=pltpu.CompilerParams(
-            collective_id=2, has_side_effects=True, vmem_limit_bytes=16 * 1024 * 1024
+            collective_id=1, has_side_effects=True, vmem_limit_bytes=16 * 1024 * 1024
         ),
         name="begin",
     )(together[:, :, : 2 * slot], coarse_inverse)
@@ -577,75 +627,42 @@
     basis = jnp.concatenate([wide * mask, spread, jnp.zeros((subs, 8, interface), f32)], axis=1)
 
     vector = jax.ShapeDtypeStruct((subs, loads, interface), f32)
-    small = jax.ShapeDtypeStruct((loads, 128), f32)
-
-    def operate(search):
-        return pl.pallas_call(
-            functools.partial(operate_kernel, nsub, lookup),
-            out_shape=(vector, small),
-            in_specs=[anywhere, vmem, vmem],
-            out_specs=(vmem, vmem),
-            scratch_shapes=[
-                pltpu.VMEM((subs, rows, interface), f32),
-                pltpu.VMEM((subs, 4, loads, interface), f32),
-                pltpu.VMEM((subs, 4, loads, rows), f32),
-                pltpu.VMEM((subs, loads, interface), f32),
-                pltpu.VMEM((2, subs, loads, slot), f32),
-                dma((subs,)),
-                dma((3, subs)),
-                dma((3, subs)),
-                dma((3, subs)),
-                dma((3, subs)),
-                dma((subs,)),
-                dma((2,)),
-                dma((2,)),
-            ],
-            compiler_params=pltpu.CompilerParams(
-                collective_id=0, has_side_effects=True, vmem_limit_bytes=48 * 1024 * 1024
-            ),
-            name="operate",
-        )(schur_block, search, mask)
-
-    def lift(v, extra):
-        out, total = pl.pallas_call(
-            functools.partial(project_kernel, nsub),
-            out_shape=(vector, small),
-            in_specs=[vmem] * 5,
-            out_specs=(vmem, vmem),
-            scratch_shapes=[
-                pltpu.VMEM((loads, 128), f32),
-                pltpu.VMEM((nsub, loads, 128), f32),
-                dma((nsub,)),
-                dma((nsub,)),
-            ],
-            compiler_params=pltpu.CompilerParams(
-                collective_id=1, has_side_effects=True, vmem_limit_bytes=32 * 1024 * 1024
-            ),
-            name="lift",
-        )(v, extra, wide, solver, basis)
-        return out, total[:, 64:65]
-
-    def dots(a, b):
-        return jnp.broadcast_to(jnp.sum(a * b, axis=(0, 2))[:, None], (loads, 128))
-
-    lifted, _ = lift(residual, jnp.zeros((loads, 128), f32))
-    projected = residual - lifted
-    scaled = precond * projected
-    lifted, energy = lift(scaled, 0.5 * dots(projected, scaled))
-    search = scaled - lifted
-    multipliers = None
-    for iteration in range(ITERS):
-        image, curve = operate(search)
-        lifted, curve = lift(image, curve)
-        step = energy / curve
-        moved = step[None] * search
-        multipliers = moved if multipliers is None else multipliers + moved
-        projected = projected - step[None] * (image - lifted)
-        if iteration + 1 < ITERS:
-            scaled = precond * projected
-            lifted, energy_new = lift(scaled, 0.5 * dots(projected, scaled))
-            search = scaled - lifted + (energy_new / energy)[None] * search
-            energy = energy_new
+
+    each_operate = [
+        pltpu.VMEM((subs, 4, loads, interface), f32),
+        pltpu.VMEM((subs, loads, interface), f32),
+        pltpu.VMEM((2, subs, loads, slot), f32),
+        dma((3, subs)),
+        dma((3, subs)),
+        dma((3, subs)),
+        dma((3, subs)),
+        dma((subs,)),
+        dma((2,)),
+        dma((2,)),
+    ]
+    each_lift = [pltpu.VMEM((nsub, loads, 128), f32), dma((nsub,)), dma((nsub,))]
+    held = pltpu.VMEM((subs, loads, interface), f32)
+    multipliers, projected = pl.pallas_call(
+        functools.partial(main_kernel, nsub, lookup),
+        out_shape=(vector, vector),
+        in_specs=[anywhere] + [vmem] * 6,
+        out_specs=(vmem, vmem),
+        scratch_shapes=[
+            pltpu.VMEM((subs, rows, interface), f32),
+            pltpu.VMEM((subs, 4, loads, rows), f32),
+            held,
+            held,
+            held,
+            pltpu.VMEM((loads, 128), f32),
+            dma((subs,)),
+        ]
+        + each_operate * ITERS
+        + each_lift * (2 * ITERS + 1),
+        compiler_params=pltpu.CompilerParams(
+            collective_id=0, has_side_effects=True, vmem_limit_bytes=48 * 1024 * 1024
+        ),
+        name="main",
+    )(schur_block, residual, precond, mask, wide, solver, basis)
     return (jnp.swapaxes(multipliers, 0, 1), jnp.swapaxes(projected, 0, 1))
 
 

time: 118 us -> 108 us (0.915)
  Pallas kernels: 104 us -> 95.3 us
  other arithmetic: 3.29 us -> 1.57 us
    pallas_call x7 -> x1, Pallas kernels: 94.8 us -> 86.1 us  [by_kernels(): pl.pallas_call(functools.partial(main_kernel, nsub, lookup), out_shape=(v...]
    unnamed x19 -> x18, local copies, waits for them, and re-layouts: 5.99 us -> 6 us
where the time goes in v2:
time: 108 us; the launch traced here: 107 us
  Pallas kernels  95.3 us (88%)
  local copies, waits for them, and re-layouts  7.89 us (7%)
  matrix products  1.67 us (2%)
  other arithmetic  1.57 us (1%)
    pallas_call x1, Pallas kernels, by_kernels(): pl.pallas_call(functools.partial(main_kernel, nsub, lookup), out_shape=(v...  86.1 us
    pallas_call x1, Pallas kernels, by_kernels(): pl.pallas_call(functools.partial(begin_kernel, nsub), out_shape=(jax.Shap...  9.21 us
    unnamed x18, local copies, waits for them, and re-layouts  6 us

profile of v2, /device:TPU:0, one launch (start us, length us, event | category | flops | bytes accessed | tf_op | source)
XLA Modules:
  0.0 107.4 jit_solution(14836902978536937070)
XLA Ops:
  0.6 0.0 copy-start.2
  0.7 0.1 pad.16.clone
  0.8 0.8 copy.16
  1.6 0.1 broadcast_in_dim.6
  1.7 0.8 broadcast_in_dim.7
  2.5 0.1 compare_convert_fusion.usable
  2.6 0.8 broadcast_bitcast_fusion
  3.4 0.0 copy-start.3
  3.4 1.2 %copy.18 = f32[8,6,1536]{2,1,0:T(8,128)S(1)} copy(f32[8,6,1536]{2,0,1:T(8,128)} %param.10) | data formatting | bytes 589824 | tf_op args[1]
  4.6 1.2 %copy.28 = f32[8,8,1536]{2,0,1:T(8,128)S(1)} copy(f32[8,8,1536]{2,1,0:T(8,128)} %param.12) | data formatting | bytes 786432 | tf_op args[3]
  5.9 0.1 pad_maximum_fusion
  6.1 9.2 %begin.1 = (f32[2,8,16,256]{3,2,1,0:T(8,128)S(1)}, f32[4,96,384]{2,1,0:T(8,128)S(1)}) custom-call(f32[8,16,512]{2,1,0:T(8,128)S(1)} %slice.167.edges, f32[96,384]{1,0:T(8,128)S(1)} %copy-done), custom_call_target="tpu_custom_call" | custom-call | tf_op jit(solution)/shard_map/begin/pallas_call | solution.py:580
  15.3 0.1 pad_dynamic-slice_fusion.1
  15.4 0.7 fusion.1
  16.1 1.0 fusion.13.solver
  17.5 0.6 copy-done.4
  18.1 0.1 compare_select_fusion.precond
  18.3 0.1 copy-done.1
  18.3 0.3 broadcast_multiply_fusion
  18.7 0.3 bitcast_multiply_fusion
  19.0 0.4 maximum_maximum_fusion.basis
  19.4 86.1 %main.1 = (f32[8,8,1536]{2,1,0:T(8,128)S(1)}, f32[8,8,1536]{2,1,0:T(8,128)S(1)}) custom-call(f32[8,384,1536]{2,1,0:T(8,128)} %schur.1, f32[8,8,1536]{2,1,0:T(8,128)S(1)} %get-tuple-element.23.residual, f32[8,1,1536]{2,1,0:T(1,128)S(1)} %compare_select_fusion.precond, f32[8,1,1536]{2,1,0:T(1,128)S(1)} %compare_convert_fusion.usable, ...), custom_call_target="tpu_custom_call" | custom-call | tf_op jit(solution)/shard_map/main/pallas_call | solution.py:645
  105.5 1.0 copy.21
  106.4 1.0 copy.22
  (33 shorter events, 0.4 us)
Async XLA Ops:
  0.6 14.7 %copy-start.2 = (f32[384,512]{1,0:T(8,128)S(1)}, f32[384,512]{1,0:T(8,128)}, u32[]{:S(2)}) copy-start(f32[384,512]{1,0:T(8,128)} %constant.49.clone) | copy-start | bytes 2359300
  0.6 5.4 %copy-start = (f32[96,384]{1,0:T(8,128)S(1)}, f32[96,384]{1,0:T(8,128)}, u32[]{:S(2)}) copy-start(f32[96,384]{1,0:T(8,128)} %block.1) | copy-start | bytes 442372
  3.4 12.7 %copy-start.3 = (f32[512,144]{1,0:T(8,128)S(1)}, f32[512,144]{1,0:T(8,128)}, u32[]{:S(2)}) copy-start(f32[512,144]{1,0:T(8,128)} %constant.50.clone) | copy-start | bytes 884740
  17.3 0.8 copy-start.4
  17.3 1.0 copy-start.1
